TPU v7x, 256 devices: a whole 4x4x8 slice. The times are simulated.
256 devices in a mesh: row: 16 (over x_lo, z), col: 16 (over x_hi, y, core).
Axes of the slice: x: 4 (x_hi: 2, x_lo: 2; x = x_hi * 2 + x_lo), y: 4, z: 8, core: 2. Of those that a mesh axis runs over, the one named last changes fastest.
Arguments:
- ham_blocks: bfloat16 [128, 4, 128, 128], P('row'), may hold values from -0.25 to 0.25
- ham_index: int32 [128, 4], P('row'), may hold values from -1 to 127, as said below
- coef_blocks: bfloat16 [64, 16, 128, 128], P('col', 'row'), may hold values from -0.5 to 0.5
- coef_index: int32 [64, 16], P('col', 'row'), may hold values from 0 to 127, as said below
- slab_blocks: bfloat16 [16, 16, 128, 128], P('row', 'col'), may hold values from -0.5 to 0.5
- slab_index: int32 [16, 16], P('row', 'col'), may hold values from 0 to 127, as said below
- pattern_index: int32 [16, 32], P('row', 'col'), may hold values from 0 to 63, as said below
Outputs:
- reduced_blocks: bfloat16 [16, 32, 128, 128], P('row', 'col')
Inputs may be any that keep to these rules, and one draw needn't show every extreme that they name: `ham_index`: each row lists its stored block columns first, all distinct, then -1 in every unused slot; a row holds 1 to 4 stored blocks, some row holds 4 and some row only one. `coef_index`: each row names 16 distinct orbital blocks. `slab_index`: each row names 16 distinct orbital blocks. `pattern_index`: entry k of a row names a block among (k // 2) * 4 to (k // 2) * 4 + 3.
All inputs are finite; a program needn't handle non-finite values.
Results may differ from a plain program's by a relative error of at most 0.0049.
Values may be sent and summed in bfloat16 or wider, within the bound.
No kernel may reach another device: no remote copies, remote signals or barrier semaphores. Data moves between devices by JAX's collectives and lax.ppermute only.
A program may use at most 128 MiB of HBM per device.

v0:
```python
import jax
import jax.numpy as jnp
from jax import lax
from jax.sharding import PartitionSpec as P


def panel_images(ham_part, index_part, column_vals, column_index):

    def one_row(row_item):
        block_row, index_row = row_item
        matches = (column_index[None, :, :] == index_row[:, None, None]).astype(jnp.bfloat16)
        columns = jnp.einsum(
            "kjm,jmab->kbja", matches, column_vals, preferred_element_type=jnp.float32
        ).astype(jnp.bfloat16)
        return jnp.einsum(
            "kxb,kbja->xja", block_row, columns, preferred_element_type=jnp.float32
        ).astype(jnp.bfloat16)

    row_total = ham_part.shape[0]
    return lax.map(one_row, (ham_part, index_part), batch_size=min(8, row_total))


def pick_image(where_row, wanted_row, products, offset):
    row_number = products.shape[0]
    targets = offset + jnp.arange(row_number, dtype=jnp.int32)
    matches = (where_row[:, None] == targets[None, :]).astype(jnp.bfloat16)
    columns = jnp.take(products, wanted_row, axis=2)
    return jnp.einsum("mn,nbkc->mbkc", matches, columns, preferred_element_type=jnp.float32)


def contract_row(coef_row, chosen):
    return jnp.einsum("mab,mbkc->kac", coef_row, chosen, preferred_element_type=jnp.float32)


def shards(ham_blocks, ham_index, coef_blocks, coef_index, slab_blocks, slab_index, pattern_index):
    column_vals, column_index = (
        lax.all_gather(coef_blocks, "row", axis=1, tiled=True),
        lax.all_gather(coef_index, "row", axis=1, tiled=True),
    )
    slab_vals, slab_where = (
        lax.all_gather(slab_blocks, "col", axis=1, tiled=True),
        lax.all_gather(slab_index, "col", axis=1, tiled=True),
    )
    col_blocks = coef_blocks.shape[0]
    block_size = coef_blocks.shape[2]
    column_pos = pattern_index - lax.axis_index("col") * col_blocks
    slab_count = slab_vals.shape[0]
    stored = slab_vals.shape[1]
    wanted_count = column_pos.shape[1]
    initial = jnp.zeros((slab_count, stored, block_size, wanted_count, block_size), jnp.float32)
    offset = jnp.int32(0)
    products = panel_images(
        lax.all_gather(ham_blocks, "row", axis=0, tiled=True),
        lax.all_gather(ham_index, "row", axis=0, tiled=True),
        column_vals,
        column_index,
    )

    def select_row(row_item):
        return pick_image(row_item[0], row_item[1], products, offset)

    chosen_all = initial + lax.map(select_row, (slab_where, column_pos))

    def finish_row(row_item):
        return contract_row(row_item[0], row_item[1].astype(jnp.bfloat16))

    result = lax.map(finish_row, (slab_vals, chosen_all))
    return result.astype(jnp.bfloat16)


def solution(mesh):
    placed = (
        P("row", None, None, None),
        P("row", None),
        P("col", "row", None, None),
        P("col", "row"),
        P("row", "col", None, None),
        P("row", "col"),
        P("row", "col"),
    )
    return jax.shard_map(
        shards, mesh=mesh, in_specs=placed, out_specs=P("row", "col", None, None), check_vma=False
    )
```

profile of v0, /device:TPU:1, one launch (start us, length us, event | category | flops | bytes accessed | tf_op | source)
XLA Modules:
  0.0 392.7 jit_solution(10934278853441092370)
XLA Ops:
  6.5 0.7 all-gather.7.cloned.1.call-update
  7.3 0.7 all-gather.5.cloned.1.call-update
  8.0 30.5 %all-gather = s32[16,1,4]{2,1,0:T(1,128)S(1)} all-gather(s32[1,1,4]{2,1,0:T(1,128)} %bitcast.93), channel_id=1, replica_groups=mesh['row'=16,'col'=16] {'row'}, dimensions={0}, use_global_device_ids=true | all-gather | bytes 272 | tf_op jit(solution)/shard_map/all_gather | solution.py:38
  38.6 34.4 %all_gather.23 = bf16[1,16,128,128]{3,2,0,1:T(8,128)(2,1)S(1)} all-gather(bf16[1,1,128,128]{3,2,0,1:T(8,128)(2,1)} %bitcast.91), channel_id=1, replica_groups=mesh['row'=16,'col'=16] {'col'}, dimensions={1}, use_global_device_ids=true | all-gather | bytes 557056 | tf_op jit(solution)/shard_map/all_gather | solution.py:41
  74.1 1.3 dynamic-slice.5
  76.0 6.4 %all-reduce = s32[16]{0:T(128)S(1)} all-reduce(s32[16]{0:T(128)S(1)} %bitcast_dynamic-update-slice_fusion.1), channel_id=1, replica_groups=mesh['row'=16,'col'=16] {'col'}, use_global_device_ids=true, to_apply=%add | all-reduce | flops 16 | bytes 128
  82.4 24.5 %all-gather.1 = s32[16,8,4]{1,2,0:T(4,128)S(1)} all-gather(s32[1,8,4]{1,2,0:T(4,128)} %bitcast.92), channel_id=1, replica_groups=mesh['row'=16,'col'=16] {'row'}, dimensions={0}, use_global_device_ids=true | all-gather | bytes 2176 | tf_op jit(solution)/shard_map/all_gather | solution.py:54
  108.2 3.0 copy.27
  111.2 157.5 %all-gather.5.cloned.1.call-done = bf16[128,4,128,128]{3,2,1,0:T(8,128)(2,1)} async-done(((bf16[8,4,128,128]{3,2,1,0:T(8,128)(2,1)}), bf16[128,4,128,128]{3,2,1,0:T(8,128)(2,1)}) %all-gather.5.cloned.1.call-update) | async-done | bytes 16777232 | tf_op jit(solution)/shard_map/all_gather | solution.py:53
  268.7 85.2 %while.3 = (s32[]{:T(128)}, bf16[16,8,128,4,128]{4,2,1,0,3:T(8,128)(2,1)}, bf16[16,8,4,128,128]{4,3,2,1,0:T(8,128)(2,1)}, s32[4,16]{1,0:T(4,128)S(1)}, s32[16,8,...) while((s32[]{:T(128)}, bf16[16,8,128,4,128]{4,2,1,0,3:T(8,128)(2,1)}, ...), condition=%wide.region_1.2_spmd, body=%wide.region_0.1_spmd.sunk | while | flops 606603264 | bytes 14680801 | solution.py:20
  268.7 1.3 convert_bitcast_fusion.2
  269.9 2.8 fusion.47
  272.7 1.2 copy_dynamic-update-slice_fusion.2
  274.0 1.3 convert_bitcast_fusion.2
  275.3 2.8 fusion.47
  278.1 1.3 copy_dynamic-update-slice_fusion.2
  279.3 1.3 convert_bitcast_fusion.2
  280.6 2.8 fusion.47
  283.4 1.3 copy_dynamic-update-slice_fusion.2
  284.6 1.3 convert_bitcast_fusion.2
  285.9 2.8 fusion.47
  288.7 1.2 copy_dynamic-update-slice_fusion.2
  290.0 1.3 convert_bitcast_fusion.2
  291.3 2.8 fusion.47
  294.0 1.2 copy_dynamic-update-slice_fusion.2
  295.3 1.3 convert_bitcast_fusion.2
  296.6 2.8 fusion.47
  299.3 1.2 copy_dynamic-update-slice_fusion.2
  300.6 1.3 convert_bitcast_fusion.2
  301.9 2.8 fusion.47
  304.6 1.2 copy_dynamic-update-slice_fusion.2
  305.9 1.3 convert_bitcast_fusion.2
  307.2 2.8 fusion.47
  310.0 1.3 copy_dynamic-update-slice_fusion.2
  311.2 1.3 convert_bitcast_fusion.2
  312.5 2.8 fusion.47
  315.3 1.3 copy_dynamic-update-slice_fusion.2
  316.6 1.3 convert_bitcast_fusion.2
  317.8 2.8 fusion.47
  320.6 1.2 copy_dynamic-update-slice_fusion.2
  321.9 1.3 convert_bitcast_fusion.2
  323.2 2.8 fusion.47
  326.0 1.3 copy_dynamic-update-slice_fusion.2
  327.2 1.3 convert_bitcast_fusion.2
  328.5 2.8 fusion.47
  331.3 1.3 copy_dynamic-update-slice_fusion.2
  332.6 1.3 convert_bitcast_fusion.2
  333.8 2.8 fusion.47
  336.6 1.2 copy_dynamic-update-slice_fusion.2
  337.9 1.3 convert_bitcast_fusion.2
  339.1 2.8 fusion.47
  341.9 1.2 copy_dynamic-update-slice_fusion.2
  343.2 1.3 convert_bitcast_fusion.2
  344.5 2.8 fusion.47
  347.2 1.2 copy_dynamic-update-slice_fusion.2
  348.5 1.3 convert_bitcast_fusion.2
  349.8 2.8 fusion.47
  352.5 1.3 copy_dynamic-update-slice_fusion.2
  353.8 12.0 %while.8 = (s32[]{:T(128)}, bf16[128,128,4,128]{3,1,0,2:T(8,128)(2,1)}, s32[2,1]{0,1:T(1,128)S(1)}, bf16[2,128,128,128]{3,2,1,0:T(8,128)(2,1)}, s32[]{:T(128)}) while((s32[]{:T(128)}, bf16[128,128,4,128]{3,1,0,2:T(8,128)(2,1)}, s32[2,1]{0,1:T(1,128)S(1)}, bf16[2,128,128,128]{3,2,1,0:T(8,128)(2,1)}, s32[]{:T(128)}) %tuple.44), condition=%wide.while_cond, body=%wide.while_body.sunk | while | flops 2 | bytes 8389205 | solution.py:27
  354.4 5.5 %bitcast_dynamic-update-slice_fusion.3 = bf16[2,128,128,128]{3,2,1,0:T(8,128)(2,1)} fusion(bf16[2,128,128,128]{3,2,1,0:T(8,128)(2,1)} %get-tuple-element.190, s32[]{:T(128)S(6)} %copy.74, bf16[128,128,4,128]{3,1,0,2:T(8,128)(2,1)} %get-tuple-element.193, s32[]{:T(128)} %bitcast.87), kind=kLoop, calls=%fused_computation.15.clone.1 | loop fusion | bytes 8389124 | tf_op jit(solution)/shard_map/while/body/eval_jaxpr/jit(_take)/gather
  360.5 5.4 %bitcast_dynamic-update-slice_fusion.3 = bf16[2,128,128,128]{3,2,1,0:T(8,128)(2,1)} fusion(bf16[2,128,128,128]{3,2,1,0:T(8,128)(2,1)} %get-tuple-element.190, s32[]{:T(128)S(6)} %copy.74, bf16[128,128,4,128]{3,1,0,2:T(8,128)(2,1)} %get-tuple-element.193, s32[]{:T(128)} %bitcast.87), kind=kLoop, calls=%fused_computation.15.clone.1 | loop fusion | bytes 8389124 | tf_op jit(solution)/shard_map/while/body/eval_jaxpr/jit(_take)/gather
  365.8 7.5 %select_bitcast_fusion = bf16[128,128,2,128]{3,1,0,2:T(8,128)(2,1)} fusion(bf16[2,128,128,128]{3,2,1,0:T(8,128)(2,1)} %get-tuple-element.72, pred[2]{0:T(512)(128)(4,1)S(1)} %compare_and_fusion), kind=kLoop, calls=%fused_computation.19 | loop fusion | flops 4194304 | bytes 16777218 | tf_op jit(solution)/shard_map/while/body/eval_jaxpr/jit(_take)/select_n | solution.py:27
  373.3 11.8 %fusion.29 = bf16[1,2,128,128]{2,3,1,0:T(8,128)(2,1)S(1)} fusion(bf16[128,128,2,128]{3,1,0,2:T(8,128)(2,1)} %select_bitcast_fusion, bf16[1,16,128,128]{2,1,3,0:T(8,128)(2,1)S(1)} %copy.31, s32[16]{0:T(128)S(1)} %all-reduce), kind=kOutput, calls=%fused_computation.24 | convolution fusion | flops 268994560 | bytes 8978496 | tf_op jit(solution)/shard_map/while/body/eval_jaxpr/mab,mbkc->kac/dot_general | solution.py:32
  385.1 0.7 copy.32
  (29 shorter events, 3.7 us)
Async XLA Ops:
  6.5 101.7 %all-gather.7.cloned.1.call-start = ((), (), s32[]{:S(2)}) async-start(), calls=%async_computation.1 | async-start | bytes 2228224 | tf_op jit(solution)/shard_map/all_gather | solution.py:37
  7.3 261.4 %all-gather.5.cloned.1.call-start = ((), (), s32[]{:S(2)}) async-start(), calls=%async_computation | async-start | bytes 17825792 | tf_op jit(solution)/shard_map/all_gather | solution.py:53
Sparse Core Ops, SparseCore 0:
  9.1 65.0 all-gather.6
  76.0 192.6 all-gather.4
where the time goes:
time: 394 us; the launch traced here: 393 us
  waiting for transfers between devices  159 us (40%)
  blocking collectives  95.8 us (24%)
  matrix products  76.7 us (19%)
  local copies, waits for them, and re-layouts  38.1 us (10%)
  between operations  14.1 us (4%)
  other arithmetic  8.81 us (2%)
    all_gather x1, waiting for transfers between devices, shards(): lax.all_gather(ham_blocks, 'row', axis=0, tiled=True)  157 us
    dot_general x16, matrix products, one_row(): jnp.einsum('kxb,kbja->xja', block_row, columns, preferred_element_type=jn...  44.4 us
    all_gather x1, blocking collectives, shards(): lax.all_gather(slab_blocks, 'col', axis=1, tiled=True)  34.4 us
    all_gather x1, blocking collectives, shards(): lax.all_gather(coef_index, 'row', axis=1, tiled=True)  30.5 us
    all_gather x1, blocking collectives, shards(): lax.all_gather(ham_index, 'row', axis=0, tiled=True)  24.5 us
    dot_general x16, matrix products, one_row(): jnp.einsum('kjm,jmab->kbja', matches, column_vals, preferred_element_type...  20.5 us
    dynamic_update_slice x16, local copies, waits for them, and re-layouts, panel_images(): lax.map(one_row, (ham_part, index_part), batch_size=min(8, row_total))  20 us
    gather x4, local copies, waits for them, and re-layouts  12 us
  transfers between devices with their start and end apart: 2, of which 1 were waited for; matrix products, arithmetic and copies ran while one was open for 2% of the time, Pallas kernels for 0%

commit v1 on v0

--- a/solution.py
+++ b/solution.py
@@ -35,7 +35,9 @@
 def shards(ham_blocks, ham_index, coef_blocks, coef_index, slab_blocks, slab_index, pattern_index):
     column_vals, column_index = (
         lax.all_gather(coef_blocks, "row", axis=1, tiled=True),
-        lax.all_gather(coef_index, "row", axis=1, tiled=True),
+        jnp.concatenate(
+            lax.all_to_all(jnp.stack([coef_index] * lax.axis_size("row")), "row", 0, 0), axis=1
+        ),
     )
     slab_vals, slab_where = (
         lax.all_gather(slab_blocks, "col", axis=1, tiled=True),

time: 394 us -> 394 us (level)
  blocking collectives: 95.8 us -> 66.9 us
  waiting for transfers between devices: 159 us -> 176 us
  starting transfers between devices: 0.04 us -> 10.1 us
    all_gather x1 -> x0, blocking collectives: 30.5 us -> none  [shards(): lax.all_gather(coef_index, 'row', axis=1, tiled=True)]
    all_gather x1, waiting for transfers between devices: 157 us -> 175 us  [shards(): lax.all_gather(ham_blocks, 'row', axis=0, tiled=True)]
    all_to_all x0 -> x1, starting transfers between devices: none -> 10 us  [shards(): lax.all_to_all(jnp.stack([coef_index] * lax.axis_size('row')), 'row', 0, 0)]
    all_gather x1, blocking collectives: 34.4 us -> 29.3 us  [shards(): lax.all_gather(slab_blocks, 'col', axis=1, tiled=True)]
    unnamed x1, blocking collectives: 6.41 us -> 11.3 us
  transfers between devices with their start and end apart: 2 -> 3, of which waited for: 1 -> 1; matrix products, arithmetic and copies ran while one was open for 2% -> 2% of each run, Pallas kernels for 0% -> 0%
where the time goes in v1:
time: 394 us; the launch traced here: 393 us
  waiting for transfers between devices  176 us (45%)
  matrix products  76.7 us (19%)
  blocking collectives  66.9 us (17%)
  local copies, waits for them, and re-layouts  39.4 us (10%)
  between operations  14.1 us (4%)
  starting transfers between devices  10.1 us (3%)
  other arithmetic  8.81 us (2%)
    all_gather x1, waiting for transfers between devices, shards(): lax.all_gather(ham_blocks, 'row', axis=0, tiled=True)  175 us
    dot_general x16, matrix products, one_row(): jnp.einsum('kxb,kbja->xja', block_row, columns, preferred_element_type=jn...  44.4 us
    all_gather x1, blocking collectives, shards(): lax.all_gather(slab_blocks, 'col', axis=1, tiled=True)  29.3 us
    all_gather x1, blocking collectives, shards(): lax.all_gather(ham_index, 'row', axis=0, tiled=True)  26.3 us
    dot_general x16, matrix products, one_row(): jnp.einsum('kjm,jmab->kbja', matches, column_vals, preferred_element_type...  20.5 us
    dynamic_update_slice x16, local copies, waits for them, and re-layouts, panel_images(): lax.map(one_row, (ham_part, index_part), batch_size=min(8, row_total))  20 us
    gather x4, local copies, waits for them, and re-layouts  12 us
    dot_general x1, matrix products, contract_row(): jnp.einsum('mab,mbkc->kac', coef_row, chosen, preferred_element_type=jnp....  11.8 us
  transfers between devices with their start and end apart: 3, of which 1 were waited for; matrix products, arithmetic and copies ran while one was open for 2% of the time, Pallas kernels for 0%

profile of v1, /device:TPU:1, one launch (start us, length us, event | category | flops | bytes accessed | tf_op | source)
XLA Modules:
  0.0 392.6 jit_solution(12456356302705964223)
XLA Ops:
  6.5 0.7 all-gather.6.cloned.1.call-update
  8.0 1.3 stack.2
  9.3 10.0 %all-to-all-start = ((s32[16,4,1]{1,2,0:T(1,128)}), s32[16,4,1]{1,2,0:T(1,128)S(1)}, u32[]{:S(2)}, u32[]{:S(2)}) async-start(s32[16,4,1]{1,2,0:T(1,128)} %stack.2), calls=%async_computation | async-start | bytes 16384 | tf_op jit(solution)/shard_map/all_to_all | solution.py:39
  19.3 29.3 %all_gather.19 = bf16[1,16,128,128]{3,2,0,1:T(8,128)(2,1)S(1)} all-gather(bf16[1,1,128,128]{3,2,0,1:T(8,128)(2,1)} %bitcast.92), channel_id=1, replica_groups=mesh['row'=16,'col'=16] {'col'}, dimensions={1}, use_global_device_ids=true | all-gather | bytes 557056 | tf_op jit(solution)/shard_map/all_gather | solution.py:43
  49.1 26.3 %all-gather = s32[16,8,4]{1,2,0:T(4,128)S(1)} all-gather(s32[1,8,4]{1,2,0:T(4,128)} %bitcast.94), channel_id=1, replica_groups=mesh['row'=16,'col'=16] {'row'}, dimensions={0}, use_global_device_ids=true | all-gather | bytes 2176 | tf_op jit(solution)/shard_map/all_gather | solution.py:56
  77.3 1.3 dynamic-slice.5
  79.3 11.3 %all-reduce = s32[16]{0:T(128)S(1)} all-reduce(s32[16]{0:T(128)S(1)} %bitcast_dynamic-update-slice_fusion.1), channel_id=1, replica_groups=mesh['row'=16,'col'=16] {'col'}, use_global_device_ids=true, to_apply=%add | all-reduce | flops 16 | bytes 128
  90.6 2.9 copy.25
  93.6 175.0 %all-gather.4.cloned.1.call-done = bf16[128,4,128,128]{3,2,1,0:T(8,128)(2,1)} async-done(((bf16[8,4,128,128]{3,2,1,0:T(8,128)(2,1)}), bf16[128,4,128,128]{3,2,1,0:T(8,128)(2,1)}) %all-gather.4.cloned.1.call-update) | async-done | bytes 16777232 | tf_op jit(solution)/shard_map/all_gather | solution.py:55
  268.6 85.1 %while.3 = (s32[]{:T(128)}, bf16[16,8,128,4,128]{4,2,1,0,3:T(8,128)(2,1)}, bf16[16,8,4,128,128]{4,3,2,1,0:T(8,128)(2,1)}, s32[4,16,1]{1,0,2:T(4,128)S(1)}, s32[1...) while((s32[]{:T(128)}, bf16[16,8,128,4,128]{4,2,1,0,3:T(8,128)(2,1)}, ...), condition=%wide.region_1.2_spmd, body=%wide.region_0.1_spmd.sunk | while | flops 606603264 | bytes 14680801 | solution.py:20
  268.6 1.3 convert_bitcast_fusion.2
  269.9 2.8 fusion.47
  272.7 1.2 copy_dynamic-update-slice_fusion.2
  273.9 1.3 convert_bitcast_fusion.2
  275.2 2.8 fusion.47
  278.0 1.3 copy_dynamic-update-slice_fusion.2
  279.2 1.3 convert_bitcast_fusion.2
  280.5 2.8 fusion.47
  283.3 1.3 copy_dynamic-update-slice_fusion.2
  284.6 1.3 convert_bitcast_fusion.2
  285.9 2.8 fusion.47
  288.6 1.2 copy_dynamic-update-slice_fusion.2
  289.9 1.3 convert_bitcast_fusion.2
  291.2 2.8 fusion.47
  293.9 1.2 copy_dynamic-update-slice_fusion.2
  295.2 1.3 convert_bitcast_fusion.2
  296.5 2.8 fusion.47
  299.3 1.2 copy_dynamic-update-slice_fusion.2
  300.5 1.3 convert_bitcast_fusion.2
  301.8 2.8 fusion.47
  304.6 1.2 copy_dynamic-update-slice_fusion.2
  305.8 1.3 convert_bitcast_fusion.2
  307.1 2.8 fusion.47
  309.9 1.3 copy_dynamic-update-slice_fusion.2
  311.1 1.3 convert_bitcast_fusion.2
  312.4 2.8 fusion.47
  315.2 1.3 copy_dynamic-update-slice_fusion.2
  316.5 1.3 convert_bitcast_fusion.2
  317.8 2.8 fusion.47
  320.5 1.2 copy_dynamic-update-slice_fusion.2
  321.8 1.3 convert_bitcast_fusion.2
  323.1 2.8 fusion.47
  325.9 1.2 copy_dynamic-update-slice_fusion.2
  327.1 1.3 convert_bitcast_fusion.2
  328.4 2.8 fusion.47
  331.2 1.3 copy_dynamic-update-slice_fusion.2
  332.4 1.3 convert_bitcast_fusion.2
  333.7 2.8 fusion.47
  336.5 1.2 copy_dynamic-update-slice_fusion.2
  337.7 1.3 convert_bitcast_fusion.2
  339.0 2.8 fusion.47
  341.8 1.2 copy_dynamic-update-slice_fusion.2
  343.0 1.3 convert_bitcast_fusion.2
  344.3 2.8 fusion.47
  347.1 1.2 copy_dynamic-update-slice_fusion.2
  348.4 1.3 convert_bitcast_fusion.2
  349.6 2.8 fusion.47
  352.4 1.3 copy_dynamic-update-slice_fusion.2
  353.7 12.0 %while.8 = (s32[]{:T(128)}, bf16[128,128,4,128]{3,1,0,2:T(8,128)(2,1)}, s32[2,1]{0,1:T(1,128)S(1)}, bf16[2,128,128,128]{3,2,1,0:T(8,128)(2,1)}, s32[]{:T(128)}) while((s32[]{:T(128)}, bf16[128,128,4,128]{3,1,0,2:T(8,128)(2,1)}, s32[2,1]{0,1:T(1,128)S(1)}, bf16[2,128,128,128]{3,2,1,0:T(8,128)(2,1)}, s32[]{:T(128)}) %tuple.45), condition=%wide.while_cond, body=%wide.while_body.sunk | while | flops 2 | bytes 8389205 | solution.py:27
  354.3 5.5 %bitcast_dynamic-update-slice_fusion.3 = bf16[2,128,128,128]{3,2,1,0:T(8,128)(2,1)} fusion(bf16[2,128,128,128]{3,2,1,0:T(8,128)(2,1)} %get-tuple-element.196, s32[]{:T(128)S(6)} %copy.72, bf16[128,128,4,128]{3,1,0,2:T(8,128)(2,1)} %get-tuple-element.199, s32[]{:T(128)} %bitcast.88), kind=kLoop, calls=%fused_computation.15.clone.1 | loop fusion | bytes 8389124 | tf_op jit(solution)/shard_map/while/body/eval_jaxpr/jit(_take)/gather
  360.3 5.4 %bitcast_dynamic-update-slice_fusion.3 = bf16[2,128,128,128]{3,2,1,0:T(8,128)(2,1)} fusion(bf16[2,128,128,128]{3,2,1,0:T(8,128)(2,1)} %get-tuple-element.196, s32[]{:T(128)S(6)} %copy.72, bf16[128,128,4,128]{3,1,0,2:T(8,128)(2,1)} %get-tuple-element.199, s32[]{:T(128)} %bitcast.88), kind=kLoop, calls=%fused_computation.15.clone.1 | loop fusion | bytes 8389124 | tf_op jit(solution)/shard_map/while/body/eval_jaxpr/jit(_take)/gather
  365.7 7.5 %select_bitcast_fusion = bf16[128,128,2,128]{3,1,0,2:T(8,128)(2,1)} fusion(bf16[2,128,128,128]{3,2,1,0:T(8,128)(2,1)} %get-tuple-element.72, pred[2]{0:T(512)(128)(4,1)S(1)} %compare_and_fusion), kind=kLoop, calls=%fused_computation.19 | loop fusion | flops 4194304 | bytes 16777218 | tf_op jit(solution)/shard_map/while/body/eval_jaxpr/jit(_take)/select_n | solution.py:27
  373.2 11.8 %fusion.29 = bf16[1,2,128,128]{2,3,1,0:T(8,128)(2,1)S(1)} fusion(bf16[128,128,2,128]{3,1,0,2:T(8,128)(2,1)} %select_bitcast_fusion, bf16[1,16,128,128]{2,1,3,0:T(8,128)(2,1)S(1)} %copy.29, s32[16]{0:T(128)S(1)} %all-reduce), kind=kOutput, calls=%fused_computation.24 | convolution fusion | flops 268994560 | bytes 8978496 | tf_op jit(solution)/shard_map/while/body/eval_jaxpr/mab,mbkc->kac/dot_general | solution.py:32
  385.0 0.7 copy.30
  (31 shorter events, 4.4 us)
Async XLA Ops:
  6.5 84.1 %all-gather.6.cloned.1.call-start = ((), (), s32[]{:S(2)}) async-start(), calls=%async_computation.2 | async-start | bytes 2228224 | tf_op jit(solution)/shard_map/all_gather | solution.py:37
  7.3 261.3 %all-gather.4.cloned.1.call-start = ((), (), s32[]{:S(2)}) async-start(), calls=%async_computation.1 | async-start | bytes 17825792 | tf_op jit(solution)/shard_map/all_gather | solution.py:55
  9.3 81.3 %all-to-all-start = ((s32[16,4,1]{1,2,0:T(1,128)}), s32[16,4,1]{1,2,0:T(1,128)S(1)}, u32[]{:S(2)}, u32[]{:S(2)}) async-start(s32[16,4,1]{1,2,0:T(1,128)} %stack.2), calls=%async_computation | async-start | bytes 16384 | tf_op jit(solution)/shard_map/all_to_all | solution.py:39
Sparse Core Ops, SparseCore 0:
  9.1 65.3 all-gather.5
  76.3 192.2 all-gather.3
